TPU v7x, 128 devices: a whole 4x4x4 slice. The times are simulated.
128 devices in a mesh: dp: 8 (over y_hi, z), ctx: 16 (over y_lo, x, core).
Axes of the slice: x: 4, y: 4 (y_hi: 2, y_lo: 2; y = y_hi * 2 + y_lo), z: 4, core: 2. Of those that a mesh axis runs over, the one named last changes fastest.
Arguments:
- hidden: bfloat16 [8, 4096, 8192], P('dp', 'ctx'), may hold values from -6 to 6
- queries: bfloat16 [8, 4096, 4096], P('dp', 'ctx')
- layout: int32 [8, 32], P('dp'), may hold values from 0 to 31, each once within a row
- boundary: int32 [8], P('dp'), may hold values from 1 to 4095
- key_matrix: bfloat16 [8192, 512], P(('dp', 'ctx')), may hold values from -0.0625 to 0.0625
- value_matrix: bfloat16 [8192, 512], P(('dp', 'ctx')), may hold values from -0.0625 to 0.0625
Outputs:
- attended: bfloat16 [8, 4096, 4096], P('dp', 'ctx')
Inputs may be any that keep to these rules, and one draw needn't show every extreme that they name: Each row holds every block number of 0 to 31 once; local block b of ctx index c is layout[2 c + b].
All inputs are finite; a program needn't handle non-finite values.
Results may differ from a plain program's by a relative error of at most 0.011.
Values may be sent and summed in bfloat16 or wider, within the bound.
A program may use at most 320 MiB of HBM per device.

v0:
```python
import jax
import jax.numpy as jnp
from jax import lax
from jax.sharding import PartitionSpec as P

HEAD_WIDTH = 128


def shifted(shard, axis, by):
    size = lax.axis_size(axis)
    return lax.ppermute(shard, axis, [(i, (i + by) % size) for i in range(size)])


def per_device(hidden, queries, layout, boundary, key_matrix, value_matrix):
    rows = hidden.shape[1]
    kv_width = key_matrix.shape[1]
    head_size = HEAD_WIDTH
    kv_heads = kv_width // head_size
    group_size = queries.shape[2] // kv_width
    half = rows // 2
    scale = head_size ** (-0.5)
    ctx_count = lax.axis_size("ctx")
    here = lax.axis_index("ctx")
    tokens = hidden[0]
    order = layout[0]
    start_doc = boundary[0]
    block_ids = jnp.arange(order.shape[0], dtype=jnp.int32)

    def positions(first, count):
        index = first + jnp.arange(count, dtype=jnp.int32)
        match = (index // half)[:, None] == block_ids[None, :]
        looked = jnp.sum(jnp.where(match, order[None, :], 0), axis=1)
        return looked * half + index % half

    keys_full = jnp.dot(
        tokens,
        lax.all_gather(key_matrix, ("dp", "ctx"), axis=0, tiled=True),
        preferred_element_type=jnp.float32,
    )
    values_full = jnp.dot(
        tokens,
        lax.all_gather(value_matrix, ("dp", "ctx"), axis=0, tiled=True),
        preferred_element_type=jnp.float32,
    )
    stacked = jnp.stack((keys_full.astype(jnp.bfloat16), values_full.astype(jnp.bfloat16)), axis=0)
    query_rows = queries[0].reshape(rows, kv_heads, group_size, head_size)
    query_pos = positions(here * rows, rows)

    def attend(state, block_list, first):
        count = block_list.shape[1]
        key_pos = positions(first, count)
        allowed = (key_pos[None, :] <= query_pos[:, None]) & (
            (key_pos[None, :] >= start_doc) | (query_pos[:, None] < start_doc)
        )
        running, total, summed = state
        key_row_set = block_list[0].reshape(count, kv_heads, head_size)
        value_row_set = block_list[1].reshape(count, kv_heads, head_size)
        scores = (
            jnp.einsum(
                "qgha,kga->ghqk", query_rows, key_row_set, preferred_element_type=jnp.float32
            )
            * scale
        )
        scores = jnp.where(allowed, scores, -1e30)
        peak = jnp.maximum(running, jnp.max(scores, axis=-1))
        factor = jnp.exp(running - peak)
        weights = jnp.where(allowed, jnp.exp(scores - peak[..., None]), 0.0)
        total = total * factor + jnp.sum(weights, axis=-1)
        probs = weights.astype(jnp.bfloat16)
        summed = summed * factor[..., None] + jnp.einsum(
            "ghqk,kga->ghqa", probs, value_row_set, preferred_element_type=jnp.float32
        )
        return (peak, total, summed)

    initial = (
        jnp.full((kv_heads, group_size, rows), -1e30, jnp.float32),
        jnp.zeros((kv_heads, group_size, rows), jnp.float32),
        jnp.zeros((kv_heads, group_size, rows, head_size), jnp.float32),
    )
    state = attend(initial, stacked, here * rows)

    def turn(step, carry):
        state_now, block_list = carry
        block_list = shifted(block_list, "ctx", 1)
        source = (here - step - 1) % ctx_count
        return (attend(state_now, block_list, source * rows), block_list)

    state, unused_blocks = lax.fori_loop(0, ctx_count - 1, turn, (state, stacked))
    running, total, summed = state
    result = summed / total[..., None]
    result = result.transpose(2, 0, 1, 3).reshape(rows, kv_heads * group_size * head_size)
    return result.astype(jnp.bfloat16)[None]


def solution(mesh):
    in_specs = (
        P("dp", "ctx", None),
        P("dp", "ctx", None),
        P("dp", None),
        P("dp"),
        P(("dp", "ctx"), None),
        P(("dp", "ctx"), None),
    )
    out_specs = P("dp", "ctx", None)
    return jax.shard_map(
        per_device, mesh=mesh, in_specs=in_specs, out_specs=out_specs, check_vma=False
    )
```

profile of v0, /device:TPU:1, one launch (start us, length us, event | category | flops | bytes accessed | tf_op | source)
XLA Modules:
  0.0 743.4 jit_solution(1733711466814543764)
XLA Ops:
  8.7 4.1 copy.26
  16.1 199.1 %all-gather.5.cloned.1.call-done = bf16[8192,512]{1,0:T(8,128)(2,1)} async-done(((bf16[64,512]{1,0:T(8,128)(2,1)}), bf16[8192,512]{1,0:T(8,128)(2,1)}) %all-gather.5.cloned.1.call-update) | async-done | bytes 8388624 | tf_op jit(solution)/shard_map/all_gather | solution.py:42
  215.2 7.0 fusion.39
  222.9 195.6 %all-gather.3.cloned.1.call-done = bf16[8192,512]{1,0:T(8,128)(2,1)} async-done(((bf16[64,512]{1,0:T(8,128)(2,1)}), bf16[8192,512]{1,0:T(8,128)(2,1)}) %all-gather.3.cloned.1.call-update) | async-done | bytes 8388624 | tf_op jit(solution)/shard_map/all_gather | solution.py:37
  418.5 7.0 fusion.36
  431.3 4.7 broadcast_add_fusion
  436.0 294.1 %while.23 = (s32[]{:T(128)}, f32[4,8,256]{2,1,0:T(8,128)S(1)}, f32[4,8,256]{2,1,0:T(8,128)S(1)}, f32[4,8,256,128]{3,2,1,0:T(8,128)}, bf16[2,256,512]{1,2,0:T(8,1...) while((s32[]{:T(128)}, f32[4,8,256]{2,1,0:T(8,128)S(1)}, ...), condition=%wide.region_7.8_spmd.clone, body=%wide.region_3.7_spmd.clone.sunk | while | flops 1103347456 | bytes 74720784 | solution.py:88
  438.6 5.2 collective-permute-done
  447.6 3.7 multiply_add_fusion.5
  456.6 5.2 collective-permute-done
  465.6 3.7 multiply_add_fusion.5
  474.6 5.2 collective-permute-done
  492.7 6.3 collective-permute-done
  510.7 8.4 %collective-permute-done = bf16[2,256,512]{1,2,0:T(8,128)(2,1)S(1)} collective-permute-done((bf16[2,256,512]{1,2,0:T(8,128)(2,1)S(1)}, bf16[2,256,512]{1,2,0:T(8,128)(2,1)S(1)}, u32[]{:S(2)}, u32[]{:S(2)}) %collective-permute-start) | collective-permute-done | bytes 524320 | tf_op jit(solution)/shard_map/while/body/eval_jaxpr/ppermute | solution.py:11
  529.5 9.8 %collective-permute-done = bf16[2,256,512]{1,2,0:T(8,128)(2,1)S(1)} collective-permute-done((bf16[2,256,512]{1,2,0:T(8,128)(2,1)S(1)}, bf16[2,256,512]{1,2,0:T(8,128)(2,1)S(1)}, u32[]{:S(2)}, u32[]{:S(2)}) %collective-permute-start) | collective-permute-done | bytes 524320 | tf_op jit(solution)/shard_map/while/body/eval_jaxpr/ppermute | solution.py:11
  549.6 9.8 %collective-permute-done = bf16[2,256,512]{1,2,0:T(8,128)(2,1)S(1)} collective-permute-done((bf16[2,256,512]{1,2,0:T(8,128)(2,1)S(1)}, bf16[2,256,512]{1,2,0:T(8,128)(2,1)S(1)}, u32[]{:S(2)}, u32[]{:S(2)}) %collective-permute-start) | collective-permute-done | bytes 524320 | tf_op jit(solution)/shard_map/while/body/eval_jaxpr/ppermute | solution.py:11
  569.8 9.8 %collective-permute-done = bf16[2,256,512]{1,2,0:T(8,128)(2,1)S(1)} collective-permute-done((bf16[2,256,512]{1,2,0:T(8,128)(2,1)S(1)}, bf16[2,256,512]{1,2,0:T(8,128)(2,1)S(1)}, u32[]{:S(2)}, u32[]{:S(2)}) %collective-permute-start) | collective-permute-done | bytes 524320 | tf_op jit(solution)/shard_map/while/body/eval_jaxpr/ppermute | solution.py:11
  589.9 9.8 %collective-permute-done = bf16[2,256,512]{1,2,0:T(8,128)(2,1)S(1)} collective-permute-done((bf16[2,256,512]{1,2,0:T(8,128)(2,1)S(1)}, bf16[2,256,512]{1,2,0:T(8,128)(2,1)S(1)}, u32[]{:S(2)}, u32[]{:S(2)}) %collective-permute-start) | collective-permute-done | bytes 524320 | tf_op jit(solution)/shard_map/while/body/eval_jaxpr/ppermute | solution.py:11
  610.1 9.8 %collective-permute-done = bf16[2,256,512]{1,2,0:T(8,128)(2,1)S(1)} collective-permute-done((bf16[2,256,512]{1,2,0:T(8,128)(2,1)S(1)}, bf16[2,256,512]{1,2,0:T(8,128)(2,1)S(1)}, u32[]{:S(2)}, u32[]{:S(2)}) %collective-permute-start) | collective-permute-done | bytes 524320 | tf_op jit(solution)/shard_map/while/body/eval_jaxpr/ppermute | solution.py:11
  630.2 9.8 %collective-permute-done = bf16[2,256,512]{1,2,0:T(8,128)(2,1)S(1)} collective-permute-done((bf16[2,256,512]{1,2,0:T(8,128)(2,1)S(1)}, bf16[2,256,512]{1,2,0:T(8,128)(2,1)S(1)}, u32[]{:S(2)}, u32[]{:S(2)}) %collective-permute-start) | collective-permute-done | bytes 524320 | tf_op jit(solution)/shard_map/while/body/eval_jaxpr/ppermute | solution.py:11
  650.4 9.8 %collective-permute-done = bf16[2,256,512]{1,2,0:T(8,128)(2,1)S(1)} collective-permute-done((bf16[2,256,512]{1,2,0:T(8,128)(2,1)S(1)}, bf16[2,256,512]{1,2,0:T(8,128)(2,1)S(1)}, u32[]{:S(2)}, u32[]{:S(2)}) %collective-permute-start) | collective-permute-done | bytes 524320 | tf_op jit(solution)/shard_map/while/body/eval_jaxpr/ppermute | solution.py:11
  670.5 9.8 %collective-permute-done = bf16[2,256,512]{1,2,0:T(8,128)(2,1)S(1)} collective-permute-done((bf16[2,256,512]{1,2,0:T(8,128)(2,1)S(1)}, bf16[2,256,512]{1,2,0:T(8,128)(2,1)S(1)}, u32[]{:S(2)}, u32[]{:S(2)}) %collective-permute-start) | collective-permute-done | bytes 524320 | tf_op jit(solution)/shard_map/while/body/eval_jaxpr/ppermute | solution.py:11
  690.7 9.8 %collective-permute-done = bf16[2,256,512]{1,2,0:T(8,128)(2,1)S(1)} collective-permute-done((bf16[2,256,512]{1,2,0:T(8,128)(2,1)S(1)}, bf16[2,256,512]{1,2,0:T(8,128)(2,1)S(1)}, u32[]{:S(2)}, u32[]{:S(2)}) %collective-permute-start) | collective-permute-done | bytes 524320 | tf_op jit(solution)/shard_map/while/body/eval_jaxpr/ppermute | solution.py:11
  710.8 9.8 %collective-permute-done = bf16[2,256,512]{1,2,0:T(8,128)(2,1)S(1)} collective-permute-done((bf16[2,256,512]{1,2,0:T(8,128)(2,1)S(1)}, bf16[2,256,512]{1,2,0:T(8,128)(2,1)S(1)}, u32[]{:S(2)}, u32[]{:S(2)}) %collective-permute-start) | collective-permute-done | bytes 524320 | tf_op jit(solution)/shard_map/while/body/eval_jaxpr/ppermute | solution.py:11
  (278 shorter events, 174.6 us)
Async XLA Ops:
  6.5 9.3 %copy-start.3 = (s32[1,32]{1,0:T(1,128)S(1)}, s32[1,32]{1,0:T(1,128)}, u32[]{:S(2)}) copy-start(s32[1,32]{1,0:T(1,128)} %param.10) | copy-start | bytes 388
  6.5 208.6 %all-gather.5.cloned.1.call-start = ((), (), s32[]{:S(2)}) async-start(), calls=%async_computation.1 | async-start | bytes 8454144 | tf_op jit(solution)/shard_map/all_gather | solution.py:42
  7.3 411.3 %all-gather.3.cloned.1.call-start = ((), (), s32[]{:S(2)}) async-start(), calls=%async_computation | async-start | bytes 8454144 | tf_op jit(solution)/shard_map/all_gather | solution.py:37
  425.8 5.4 copy-start.2
  436.0 7.8 %collective-permute-start = (bf16[2,256,512]{1,2,0:T(8,128)(2,1)S(1)}, bf16[2,256,512]{1,2,0:T(8,128)(2,1)S(1)}, u32[]{:S(2)}, u32[]{:S(2)}) collective-permute-start(bf16[2,256,512]{1,2,0:T(8,128)(2,1)S(1)} %get-tuple-element.491), channel_id=1, source_target_pairs={{0,1},{1,2},{2,3},{3,4},{4,5},{5,6},{6,7},{7,8},{8,9},{9,10},{10,1... | collective-permute-start | bytes 1572872 | tf_op jit(solution)/shard_map/while/body/eval_jaxpr/ppermute | solution.py:11
  443.8 3.7 copy-start
  453.2 8.6 %collective-permute-start = (bf16[2,256,512]{1,2,0:T(8,128)(2,1)S(1)}, bf16[2,256,512]{1,2,0:T(8,128)(2,1)S(1)}, u32[]{:S(2)}, u32[]{:S(2)}) collective-permute-start(bf16[2,256,512]{1,2,0:T(8,128)(2,1)S(1)} %get-tuple-element.491), channel_id=1, source_target_pairs={{0,1},{1,2},{2,3},{3,4},{4,5},{5,6},{6,7},{7,8},{8,9},{9,10},{10,1... | collective-permute-start | bytes 1572872 | tf_op jit(solution)/shard_map/while/body/eval_jaxpr/ppermute | solution.py:11
  461.9 3.7 copy-start
  471.3 8.6 %collective-permute-start = (bf16[2,256,512]{1,2,0:T(8,128)(2,1)S(1)}, bf16[2,256,512]{1,2,0:T(8,128)(2,1)S(1)}, u32[]{:S(2)}, u32[]{:S(2)}) collective-permute-start(bf16[2,256,512]{1,2,0:T(8,128)(2,1)S(1)} %get-tuple-element.491), channel_id=1, source_target_pairs={{0,1},{1,2},{2,3},{3,4},{4,5},{5,6},{6,7},{7,8},{8,9},{9,10},{10,1... | collective-permute-start | bytes 1572872 | tf_op jit(solution)/shard_map/while/body/eval_jaxpr/ppermute | solution.py:11
  479.9 3.7 copy-start
  489.3 9.7 %collective-permute-start = (bf16[2,256,512]{1,2,0:T(8,128)(2,1)S(1)}, bf16[2,256,512]{1,2,0:T(8,128)(2,1)S(1)}, u32[]{:S(2)}, u32[]{:S(2)}) collective-permute-start(bf16[2,256,512]{1,2,0:T(8,128)(2,1)S(1)} %get-tuple-element.491), channel_id=1, source_target_pairs={{0,1},{1,2},{2,3},{3,4},{4,5},{5,6},{6,7},{7,8},{8,9},{9,10},{10,1... | collective-permute-start | bytes 1572872 | tf_op jit(solution)/shard_map/while/body/eval_jaxpr/ppermute | solution.py:11
  508.4 10.7 %collective-permute-start = (bf16[2,256,512]{1,2,0:T(8,128)(2,1)S(1)}, bf16[2,256,512]{1,2,0:T(8,128)(2,1)S(1)}, u32[]{:S(2)}, u32[]{:S(2)}) collective-permute-start(bf16[2,256,512]{1,2,0:T(8,128)(2,1)S(1)} %get-tuple-element.491), channel_id=1, source_target_pairs={{0,1},{1,2},{2,3},{3,4},{4,5},{5,6},{6,7},{7,8},{8,9},{9,10},{10,1... | collective-permute-start | bytes 1572872 | tf_op jit(solution)/shard_map/while/body/eval_jaxpr/ppermute | solution.py:11
  528.6 10.7 %collective-permute-start = (bf16[2,256,512]{1,2,0:T(8,128)(2,1)S(1)}, bf16[2,256,512]{1,2,0:T(8,128)(2,1)S(1)}, u32[]{:S(2)}, u32[]{:S(2)}) collective-permute-start(bf16[2,256,512]{1,2,0:T(8,128)(2,1)S(1)} %get-tuple-element.491), channel_id=1, source_target_pairs={{0,1},{1,2},{2,3},{3,4},{4,5},{5,6},{6,7},{7,8},{8,9},{9,10},{10,1... | collective-permute-start | bytes 1572872 | tf_op jit(solution)/shard_map/while/body/eval_jaxpr/ppermute | solution.py:11
  548.7 10.7 %collective-permute-start = (bf16[2,256,512]{1,2,0:T(8,128)(2,1)S(1)}, bf16[2,256,512]{1,2,0:T(8,128)(2,1)S(1)}, u32[]{:S(2)}, u32[]{:S(2)}) collective-permute-start(bf16[2,256,512]{1,2,0:T(8,128)(2,1)S(1)} %get-tuple-element.491), channel_id=1, source_target_pairs={{0,1},{1,2},{2,3},{3,4},{4,5},{5,6},{6,7},{7,8},{8,9},{9,10},{10,1... | collective-permute-start | bytes 1572872 | tf_op jit(solution)/shard_map/while/body/eval_jaxpr/ppermute | solution.py:11
  559.5 3.7 copy-start
  568.9 10.7 %collective-permute-start = (bf16[2,256,512]{1,2,0:T(8,128)(2,1)S(1)}, bf16[2,256,512]{1,2,0:T(8,128)(2,1)S(1)}, u32[]{:S(2)}, u32[]{:S(2)}) collective-permute-start(bf16[2,256,512]{1,2,0:T(8,128)(2,1)S(1)} %get-tuple-element.491), channel_id=1, source_target_pairs={{0,1},{1,2},{2,3},{3,4},{4,5},{5,6},{6,7},{7,8},{8,9},{9,10},{10,1... | collective-permute-start | bytes 1572872 | tf_op jit(solution)/shard_map/while/body/eval_jaxpr/ppermute | solution.py:11
  589.0 10.7 %collective-permute-start = (bf16[2,256,512]{1,2,0:T(8,128)(2,1)S(1)}, bf16[2,256,512]{1,2,0:T(8,128)(2,1)S(1)}, u32[]{:S(2)}, u32[]{:S(2)}) collective-permute-start(bf16[2,256,512]{1,2,0:T(8,128)(2,1)S(1)} %get-tuple-element.491), channel_id=1, source_target_pairs={{0,1},{1,2},{2,3},{3,4},{4,5},{5,6},{6,7},{7,8},{8,9},{9,10},{10,1... | collective-permute-start | bytes 1572872 | tf_op jit(solution)/shard_map/while/body/eval_jaxpr/ppermute | solution.py:11
  599.8 3.7 copy-start
  609.2 10.7 %collective-permute-start = (bf16[2,256,512]{1,2,0:T(8,128)(2,1)S(1)}, bf16[2,256,512]{1,2,0:T(8,128)(2,1)S(1)}, u32[]{:S(2)}, u32[]{:S(2)}) collective-permute-start(bf16[2,256,512]{1,2,0:T(8,128)(2,1)S(1)} %get-tuple-element.491), channel_id=1, source_target_pairs={{0,1},{1,2},{2,3},{3,4},{4,5},{5,6},{6,7},{7,8},{8,9},{9,10},{10,1... | collective-permute-start | bytes 1572872 | tf_op jit(solution)/shard_map/while/body/eval_jaxpr/ppermute | solution.py:11
  629.3 10.7 %collective-permute-start = (bf16[2,256,512]{1,2,0:T(8,128)(2,1)S(1)}, bf16[2,256,512]{1,2,0:T(8,128)(2,1)S(1)}, u32[]{:S(2)}, u32[]{:S(2)}) collective-permute-start(bf16[2,256,512]{1,2,0:T(8,128)(2,1)S(1)} %get-tuple-element.491), channel_id=1, source_target_pairs={{0,1},{1,2},{2,3},{3,4},{4,5},{5,6},{6,7},{7,8},{8,9},{9,10},{10,1... | collective-permute-start | bytes 1572872 | tf_op jit(solution)/shard_map/while/body/eval_jaxpr/ppermute | solution.py:11
  649.5 10.7 %collective-permute-start = (bf16[2,256,512]{1,2,0:T(8,128)(2,1)S(1)}, bf16[2,256,512]{1,2,0:T(8,128)(2,1)S(1)}, u32[]{:S(2)}, u32[]{:S(2)}) collective-permute-start(bf16[2,256,512]{1,2,0:T(8,128)(2,1)S(1)} %get-tuple-element.491), channel_id=1, source_target_pairs={{0,1},{1,2},{2,3},{3,4},{4,5},{5,6},{6,7},{7,8},{8,9},{9,10},{10,1... | collective-permute-start | bytes 1572872 | tf_op jit(solution)/shard_map/while/body/eval_jaxpr/ppermute | solution.py:11
  669.6 10.7 %collective-permute-start = (bf16[2,256,512]{1,2,0:T(8,128)(2,1)S(1)}, bf16[2,256,512]{1,2,0:T(8,128)(2,1)S(1)}, u32[]{:S(2)}, u32[]{:S(2)}) collective-permute-start(bf16[2,256,512]{1,2,0:T(8,128)(2,1)S(1)} %get-tuple-element.491), channel_id=1, source_target_pairs={{0,1},{1,2},{2,3},{3,4},{4,5},{5,6},{6,7},{7,8},{8,9},{9,10},{10,1... | collective-permute-start | bytes 1572872 | tf_op jit(solution)/shard_map/while/body/eval_jaxpr/ppermute | solution.py:11
  689.8 10.7 %collective-permute-start = (bf16[2,256,512]{1,2,0:T(8,128)(2,1)S(1)}, bf16[2,256,512]{1,2,0:T(8,128)(2,1)S(1)}, u32[]{:S(2)}, u32[]{:S(2)}) collective-permute-start(bf16[2,256,512]{1,2,0:T(8,128)(2,1)S(1)} %get-tuple-element.491), channel_id=1, source_target_pairs={{0,1},{1,2},{2,3},{3,4},{4,5},{5,6},{6,7},{7,8},{8,9},{9,10},{10,1... | collective-permute-start | bytes 1572872 | tf_op jit(solution)/shard_map/while/body/eval_jaxpr/ppermute | solution.py:11
  709.9 10.7 %collective-permute-start = (bf16[2,256,512]{1,2,0:T(8,128)(2,1)S(1)}, bf16[2,256,512]{1,2,0:T(8,128)(2,1)S(1)}, u32[]{:S(2)}, u32[]{:S(2)}) collective-permute-start(bf16[2,256,512]{1,2,0:T(8,128)(2,1)S(1)} %get-tuple-element.491), channel_id=1, source_target_pairs={{0,1},{1,2},{2,3},{3,4},{4,5},{5,6},{6,7},{7,8},{8,9},{9,10},{10,1... | collective-permute-start | bytes 1572872 | tf_op jit(solution)/shard_map/while/body/eval_jaxpr/ppermute | solution.py:11
  (25 other events, 66.3 us)
Sparse Core Ops, SparseCore 0:
  9.1 206.0 all-gather.4
  216.9 201.5 all-gather.2
where the time goes:
time: 752 us; the launch traced here: 743 us
  waiting for transfers between devices  524 us (70%)
  matrix products  101 us (13%)
  other arithmetic  50.8 us (7%)
  local copies, waits for them, and re-layouts  41.2 us (5%)
  between operations  14.2 us (2%)
  starting transfers between devices  10.5 us (1%)
    all_gather x1, waiting for transfers between devices, per_device(): lax.all_gather(value_matrix, ('dp', 'ctx'), axis=0, tiled=True)  199 us
    all_gather x1, waiting for transfers between devices, per_device(): lax.all_gather(key_matrix, ('dp', 'ctx'), axis=0, tiled=True)  196 us
    ppermute x15, waiting for transfers between devices, shifted(): lax.ppermute(shard, axis, [(i, (i + by) % size) for i in range(size)])  128 us
    dot_general x16, matrix products, attend(): jnp.einsum('ghqk,kga->ghqa', probs, value_row_set, preferred_element_type...  60.5 us
    reduce_sum x16, other arithmetic, attend(): total = total * factor + jnp.sum(weights, axis=-1)  33.8 us
    while x90, local copies, waits for them, and re-layouts  28.9 us
    dot_general x16, matrix products, attend(): jnp.einsum('qgha,kga->ghqk', query_rows, key_row_set, preferred_element_t...  26.2 us
  transfers between devices with their start and end apart: 17, of which 17 were waited for; matrix products, arithmetic and copies ran while one was open for 4% of the time, Pallas kernels for 0%

commit v1 on v0

v1 whole, which is shorter than its diff:
```python
import functools

import jax
import jax.numpy as jnp
from jax import lax
from jax.experimental import pallas as pl
from jax.experimental.pallas import tpu as pltpu
from jax.sharding import PartitionSpec as P

HEAD_WIDTH = 128
KEY_TILE = 512
NEG = -1e30


def attend_kernel(flag_ref, bound_ref, q_ref, k_ref, v_ref, qp_ref, kp_ref, o_ref, m_sc, l_sc, acc_sc):
    step = pl.program_id(0)
    group_size = m_sc.shape[0]
    scale = HEAD_WIDTH ** (-0.5)

    @pl.when(step == 0)
    def _():
        m_sc[...] = jnp.full_like(m_sc, NEG)
        l_sc[...] = jnp.zeros_like(l_sc)
        acc_sc[...] = jnp.zeros_like(acc_sc)

    def update(masked):
        k = k_ref[...]
        v = v_ref[...]
        if masked:
            start = bound_ref[0]
            qp = qp_ref[...]
            kp = kp_ref[...]
            allowed = (kp <= qp) & ((kp >= start) | (qp < start))
        for j in range(group_size):
            q = q_ref[:, j * HEAD_WIDTH:(j + 1) * HEAD_WIDTH]
            s = lax.dot_general(q, k, (((1,), (1,)), ((), ())), preferred_element_type=jnp.float32) * scale
            if masked:
                s = jnp.where(allowed, s, NEG)
            m_prev = m_sc[j]
            m_new = jnp.maximum(m_prev, jnp.max(s, axis=1, keepdims=True))
            alpha = jnp.exp(m_prev - m_new)
            p = jnp.exp(s - m_new)
            l_sc[j] = alpha * l_sc[j] + jnp.sum(p, axis=1, keepdims=True)
            acc_sc[j] = alpha * acc_sc[j] + jnp.dot(
                p.astype(jnp.bfloat16), v, preferred_element_type=jnp.float32
            )
            m_sc[j] = m_new

    flag = flag_ref[step]

    @pl.when(flag == 1)
    def _():
        update(True)

    @pl.when(flag == 2)
    def _():
        update(False)

    @pl.when(step == pl.num_programs(0) - 1)
    def _():
        for j in range(group_size):
            o_ref[:, j * HEAD_WIDTH:(j + 1) * HEAD_WIDTH] = (acc_sc[j] / l_sc[j]).astype(o_ref.dtype)


def attend_group(flags, bound, queries, kv, qpos, kpos, group_size):
    rows = queries.shape[0]
    keys = kv.shape[0]
    tiles = keys // KEY_TILE
    width = group_size * HEAD_WIDTH
    flops = 4 * rows * keys * width
    return pl.pallas_call(
        functools.partial(attend_kernel),
        out_shape=jax.ShapeDtypeStruct((rows, width), jnp.bfloat16),
        grid_spec=pltpu.PrefetchScalarGridSpec(
            num_scalar_prefetch=2,
            grid=(tiles,),
            in_specs=[
                pl.BlockSpec((rows, width), lambda i, f, b: (0, 0)),
                pl.BlockSpec((KEY_TILE, HEAD_WIDTH), lambda i, f, b: (i, 0)),
                pl.BlockSpec((KEY_TILE, HEAD_WIDTH), lambda i, f, b: (i, 1)),
                pl.BlockSpec((rows, 1), lambda i, f, b: (0, 0)),
                pl.BlockSpec((1, KEY_TILE), lambda i, f, b: (0, i)),
            ],
            out_specs=pl.BlockSpec((rows, width), lambda i, f, b: (0, 0)),
            scratch_shapes=[
                pltpu.VMEM((group_size, rows, 1), jnp.float32),
                pltpu.VMEM((group_size, rows, 1), jnp.float32),
                pltpu.VMEM((group_size, rows, HEAD_WIDTH), jnp.float32),
            ],
        ),
        compiler_params=pltpu.CompilerParams(dimension_semantics=("arbitrary",)),
        cost_estimate=pl.CostEstimate(
            flops=flops,
            transcendentals=rows * keys * group_size,
            bytes_accessed=2 * (rows * width * 2 + keys * 2 * HEAD_WIDTH),
        ),
    )(flags, bound, queries, kv, kv, qpos, kpos)


def per_device(hidden, queries, layout, boundary, key_matrix, value_matrix):
    rows = hidden.shape[1]
    kv_width = key_matrix.shape[1]
    kv_heads = kv_width // HEAD_WIDTH
    group_size = queries.shape[2] // kv_width
    block = rows // 2
    ctx_count = lax.axis_size("ctx")
    dp_count = lax.axis_size("dp")
    here = lax.axis_index("ctx")
    tokens = hidden[0]
    order = layout[0]
    start_doc = boundary[0]
    window = rows * ctx_count

    kpos = (order[:, None] * block + jnp.arange(block, dtype=jnp.int32)[None, :]).reshape(window)
    qpos = lax.dynamic_slice(kpos, (here * rows,), (rows,))
    allowed = (kpos[None, :] <= qpos[:, None]) & ((kpos[None, :] >= start_doc) | (qpos[:, None] < start_doc))
    tiles = allowed.reshape(rows, window // KEY_TILE, KEY_TILE)
    some = jnp.any(tiles, axis=(0, 2))
    every = jnp.all(tiles, axis=(0, 2))
    flags = jnp.where(every, 2, jnp.where(some, 1, 0)).astype(jnp.int32)
    bound = boundary.astype(jnp.int32)
    qpos2 = qpos[:, None]
    kpos2 = kpos[None, :]

    feat = key_matrix.shape[0]
    outs = []
    for g in range(kv_heads):
        cols = slice(g * HEAD_WIDTH, (g + 1) * HEAD_WIDTH)
        w = jnp.concatenate((key_matrix[:, cols], value_matrix[:, cols]), axis=1)
        w = lax.all_gather(w, "dp", axis=0, tiled=True)
        w = lax.all_gather(w, "ctx", axis=0, tiled=True)
        w = w.reshape(ctx_count, dp_count, feat, 2 * HEAD_WIDTH)
        part = jnp.einsum(
            "tdcr,cdrn->tn",
            tokens.reshape(rows, dp_count, ctx_count, feat),
            w,
            preferred_element_type=jnp.float32,
        ).astype(jnp.bfloat16)
        kv = lax.all_gather(part, "ctx", axis=0, tiled=True)
        q_g = queries[0][:, g * group_size * HEAD_WIDTH:(g + 1) * group_size * HEAD_WIDTH]
        outs.append(attend_group(flags, bound, q_g, kv, qpos2, kpos2, group_size))
    return jnp.concatenate(outs, axis=1)[None]


def solution(mesh):
    in_specs = (
        P("dp", "ctx", None),
        P("dp", "ctx", None),
        P("dp", None),
        P("dp"),
        P(("dp", "ctx"), None),
        P(("dp", "ctx"), None),
    )
    out_specs = P("dp", "ctx", None)
    return jax.shard_map(
        per_device, mesh=mesh, in_specs=in_specs, out_specs=out_specs, check_vma=False
    )
```

time: 752 us -> 389 us (0.52); the launches traced: 743 us -> 389 us
  waiting for transfers between devices: 524 us -> 77 us
  Pallas kernels: 0 us -> 134 us
  blocking collectives: 0 us -> 124 us
  matrix products: 101 us -> 23.8 us
  other arithmetic: 50.8 us -> 5.79 us
  local copies, waits for them, and re-layouts: 41.2 us -> 9.64 us
  starting transfers between devices: 10.5 us -> 0.48 us
    all_gather x2 -> x8, waiting for transfers between devices: 395 us -> 76.9 us  [the longest x4 46.3 us: per_device(): w = lax.all_gather(w, 'ctx', axis=0, tiled=True)]
    pallas_call x0 -> x4, Pallas kernels: none -> 134 us  [attend_group(): pl.pallas_call(functools.partial(attend_kernel), out_shape=jax.ShapeDtype...]
    ppermute x15 -> x0, waiting for transfers between devices: 128 us -> none  [shifted(): lax.ppermute(shard, axis, [(i, (i + by) % size) for i in range(size)])]
    all_gather x0 -> x4, blocking collectives: none -> 124 us  [per_device(): w = lax.all_gather(w, 'dp', axis=0, tiled=True)]
    dot_general x34 -> x4, matrix products: 101 us -> 23.8 us  [per_device(): jnp.einsum('tdcr,cdrn->tn', tokens.reshape(rows, dp_count, ctx_count, fea...]
    reduce_sum x32 -> x0, other arithmetic: 35.3 us -> none  [the longest x16 33.8 us: attend(): total = total * factor + jnp.sum(weights, axis=-1)]
    while x90 -> x0, local copies, waits for them, and re-layouts: 28.9 us -> none
    ppermute x15 -> x0, starting transfers between devices: 10.5 us -> none  [shifted(): lax.ppermute(shard, axis, [(i, (i + by) % size) for i in range(size)])]
  transfers between devices with their start and end apart: 17 -> 8, of which waited for: 17 -> 6; matrix products, arithmetic and copies ran while one was open for 4% -> 9% of each run, Pallas kernels for 0% -> 26%
where the time goes in v1:
time: 389 us
  Pallas kernels  134 us (34%)
  blocking collectives  124 us (32%)
  waiting for transfers between devices  77 us (20%)
  matrix products  23.8 us (6%)
  between operations  14.2 us (4%)
  local copies, waits for them, and re-layouts  9.64 us (2%)
  other arithmetic  5.79 us (1%)
    pallas_call x4, Pallas kernels, attend_group(): pl.pallas_call(functools.partial(attend_kernel), out_shape=jax.ShapeDtype...  134 us
    all_gather x4, blocking collectives, per_device(): w = lax.all_gather(w, 'dp', axis=0, tiled=True)  124 us
    all_gather x4, waiting for transfers between devices, per_device(): w = lax.all_gather(w, 'ctx', axis=0, tiled=True)  46.3 us
    all_gather x4, waiting for transfers between devices, per_device(): kv = lax.all_gather(part, 'ctx', axis=0, tiled=True)  30.6 us
    dot_general x4, matrix products, per_device(): jnp.einsum('tdcr,cdrn->tn', tokens.reshape(rows, dp_count, ctx_count, fea...  23.8 us
  transfers between devices with their start and end apart: 8, of which 6 were waited for; matrix products, arithmetic and copies ran while one was open for 9% of the time, Pallas kernels for 26%

profile of v1, /device:TPU:1, one launch (start us, length us, event | category | flops | bytes accessed | tf_op | source)
XLA Modules:
  0.0 388.5 jit_solution(14911302585987263947)
XLA Ops:
  6.5 0.8 fusion.48
  7.4 32.4 %all_gather.36 = bf16[512,256]{1,0:T(8,128)(2,1)} all-gather(bf16[64,256]{1,0:T(8,128)(2,1)S(1)} %pad_maximum_fusion), channel_id=1, replica_groups=mesh['dp'=8,'ctx'=16] {'dp'}, dimensions={0}, use_global_device_ids=true | all-gather | bytes 294912 | tf_op jit(solution)/shard_map/all_gather | solution.py:130
  39.9 30.6 %all_gather.39 = bf16[512,256]{1,0:T(8,128)(2,1)} all-gather(bf16[64,256]{1,0:T(8,128)(2,1)S(1)} %pad_maximum_fusion.1), channel_id=1, replica_groups=mesh['dp'=8,'ctx'=16] {'dp'}, dimensions={0}, use_global_device_ids=true | all-gather | bytes 294912 | tf_op jit(solution)/shard_map/all_gather | solution.py:130
  70.6 30.2 %all_gather.42 = bf16[512,256]{1,0:T(8,128)(2,1)} all-gather(bf16[64,256]{1,0:T(8,128)(2,1)S(1)} %pad_maximum_fusion.2), channel_id=1, replica_groups=mesh['dp'=8,'ctx'=16] {'dp'}, dimensions={0}, use_global_device_ids=true | all-gather | bytes 294912 | tf_op jit(solution)/shard_map/all_gather | solution.py:130
  100.9 30.5 %all_gather.45 = bf16[512,256]{1,0:T(8,128)(2,1)} all-gather(bf16[64,256]{1,0:T(8,128)(2,1)S(1)} %pad_maximum_fusion.3), channel_id=1, replica_groups=mesh['dp'=8,'ctx'=16] {'dp'}, dimensions={0}, use_global_device_ids=true | all-gather | bytes 294912 | tf_op jit(solution)/shard_map/all_gather | solution.py:130
  131.5 6.5 %copy.29 = bf16[1,256,8192]{1,2,0:T(8,128)(2,1)} copy(bf16[1,256,8192]{2,1,0:T(8,128)(2,1)} %param.6) | data formatting | bytes 8388608 | tf_op args[0]
  138.0 6.0 %fusion.34 = bf16[256,256]{1,0:T(8,128)(2,1)} fusion(bf16[16,8,64,256]{3,2,1,0:T(8,128)(2,1)} %bitcast.69, bf16[256,8,16,64]{0,3,2,1:T(8,128)(2,1)} %bitcast.56), kind=kOutput, calls=%fused_computation.20 | convolution fusion | flops 1073807360 | bytes 8519680 | tf_op jit(solution)/shard_map/tdcr,cdrn->tn/dot_general | solution.py:133
  144.1 6.0 %fusion.37 = bf16[256,256]{1,0:T(8,128)(2,1)} fusion(bf16[16,8,64,256]{3,2,1,0:T(8,128)(2,1)} %bitcast.68, bf16[256,8,16,64]{0,3,2,1:T(8,128)(2,1)} %bitcast.57), kind=kOutput, calls=%fused_computation.21 | convolution fusion | flops 1073807360 | bytes 8519680 | tf_op jit(solution)/shard_map/tdcr,cdrn->tn/dot_general | solution.py:133
  150.2 13.6 %all-gather.17.cloned.1.call-done = bf16[8192,256]{1,0:T(8,128)(2,1)} async-done(((bf16[512,256]{1,0:T(8,128)(2,1)}), bf16[8192,256]{1,0:T(8,128)(2,1)}) %all-gather.17.cloned.1.call-update) | async-done | bytes 4194320 | tf_op jit(solution)/shard_map/all_gather | solution.py:131
  163.7 5.9 %fusion.40 = bf16[256,256]{1,0:T(8,128)(2,1)} fusion(bf16[16,8,64,256]{3,2,1,0:T(8,128)(2,1)} %bitcast.66, bf16[256,8,16,64]{0,3,2,1:T(8,128)(2,1)} %bitcast.58), kind=kOutput, calls=%fused_computation.22 | convolution fusion | flops 1073807360 | bytes 8519680 | tf_op jit(solution)/shard_map/tdcr,cdrn->tn/dot_general | solution.py:133
  169.9 32.7 %all-gather.21.cloned.1.call-done = bf16[8192,256]{1,0:T(8,128)(2,1)} async-done(((bf16[512,256]{1,0:T(8,128)(2,1)}), bf16[8192,256]{1,0:T(8,128)(2,1)}) %all-gather.21.cloned.1.call-update) | async-done | bytes 4194320 | tf_op jit(solution)/shard_map/all_gather | solution.py:131
  202.6 6.0 %fusion.43 = bf16[256,256]{1,0:T(8,128)(2,1)} fusion(bf16[16,8,64,256]{3,2,1,0:T(8,128)(2,1)} %bitcast.67, bf16[256,8,16,64]{0,3,2,1:T(8,128)(2,1)} %bitcast.59), kind=kOutput, calls=%fused_computation.23 | convolution fusion | flops 1073807360 | bytes 8519680 | tf_op jit(solution)/shard_map/tdcr,cdrn->tn/dot_general | solution.py:133
  210.2 0.8 copy.32.qp_ref
  211.0 1.8 fusion
  213.4 1.4 fusion.47
  214.8 23.4 %all-gather.11.cloned.1.call-done.k_ref.v_ref = bf16[4096,256]{1,0:T(8,128)(2,1)} async-done(((bf16[256,256]{1,0:T(8,128)(2,1)}), bf16[4096,256]{1,0:T(8,128)(2,1)}) %all-gather.11.cloned.1.call-update) | async-done | bytes 2097168 | tf_op jit(solution)/shard_map/all_gather | solution.py:139
  238.2 33.2 %shard_map.64 = bf16[256,1024]{1,0:T(8,128)(2,1)} custom-call(s32[8]{0:T(128)} %select_select_fusion.flag_ref, s32[1]{0:T(128)} %copy.82.bound_ref, bf16[256,1024]{1,0:T(8,128)(2,1)} %get-tuple-element.11.q_ref, bf16[4096,256]{1,0:T(8,128)(2,1)} %all-gather.11.cloned.1.call-done.k_ref.v_ref, bf16[4096,256]{1,0:T(8,128)(2,1)} %all-gather.11.cloned.1.call-done.k_ref.v_ref, ...), custom_call_target="tpu_custom_call" | custom-call | flops 4294967296 | bytes 3145728 | tf_op jit(solution)/shard_map/pallas_call | solution.py:71
  271.4 2.4 all-gather.15.cloned.1.call-done.k_ref.v_ref
  273.8 33.4 %shard_map.65 = bf16[256,1024]{1,0:T(8,128)(2,1)} custom-call(s32[8]{0:T(128)} %select_select_fusion.flag_ref, s32[1]{0:T(128)} %copy.82.bound_ref, bf16[256,1024]{1,0:T(8,128)(2,1)} %get-tuple-element.14.q_ref, bf16[4096,256]{1,0:T(8,128)(2,1)} %all-gather.15.cloned.1.call-done.k_ref.v_ref, bf16[4096,256]{1,0:T(8,128)(2,1)} %all-gather.15.cloned.1.call-done.k_ref.v_ref, ...), custom_call_target="tpu_custom_call" | custom-call | flops 4294967296 | bytes 3145728 | tf_op jit(solution)/shard_map/pallas_call | solution.py:71
  307.3 2.4 all-gather.19.cloned.1.call-done.k_ref.v_ref
  309.7 33.5 %shard_map.66 = bf16[256,1024]{1,0:T(8,128)(2,1)} custom-call(s32[8]{0:T(128)} %select_select_fusion.flag_ref, s32[1]{0:T(128)} %copy.82.bound_ref, bf16[256,1024]{1,0:T(8,128)(2,1)} %get-tuple-element.13.q_ref, bf16[4096,256]{1,0:T(8,128)(2,1)} %all-gather.19.cloned.1.call-done.k_ref.v_ref, bf16[4096,256]{1,0:T(8,128)(2,1)} %all-gather.19.cloned.1.call-done.k_ref.v_ref, ...), custom_call_target="tpu_custom_call" | custom-call | flops 4294967296 | bytes 3145728 | tf_op jit(solution)/shard_map/pallas_call | solution.py:71
  343.1 2.3 all-gather.23.cloned.1.call-done.k_ref.v_ref
  345.5 33.6 %shard_map.67 = bf16[256,1024]{1,0:T(8,128)(2,1)} custom-call(s32[8]{0:T(128)} %select_select_fusion.flag_ref, s32[1]{0:T(128)} %copy.82.bound_ref, bf16[256,1024]{1,0:T(8,128)(2,1)} %get-tuple-element.12.q_ref, bf16[4096,256]{1,0:T(8,128)(2,1)} %all-gather.23.cloned.1.call-done.k_ref.v_ref, bf16[4096,256]{1,0:T(8,128)(2,1)} %all-gather.23.cloned.1.call-done.k_ref.v_ref, ...), custom_call_target="tpu_custom_call" | custom-call | flops 4294967296 | bytes 3145728 | tf_op jit(solution)/shard_map/pallas_call | solution.py:71
  379.1 2.5 maximum_bitcast_fusion
  (41 shorter events, 2.3 us)
Async XLA Ops:
  6.5 131.5 %all-gather.9.cloned.1.call-start = ((), (), s32[]{:S(2)}) async-start(), calls=%async_computation | async-start | bytes 4456448 | tf_op jit(solution)/shard_map/all_gather | solution.py:131
  39.9 104.2 %all-gather.13.cloned.1.call-start = ((), (), s32[]{:S(2)}) async-start(), calls=%async_computation.2 | async-start | bytes 4456448 | tf_op jit(solution)/shard_map/all_gather | solution.py:131
  70.6 93.2 %all-gather.17.cloned.1.call-start = ((), (), s32[]{:S(2)}) async-start(), calls=%async_computation.4 | async-start | bytes 4456448 | tf_op jit(solution)/shard_map/all_gather | solution.py:131
  100.9 101.7 %all-gather.21.cloned.1.call-start = ((), (), s32[]{:S(2)}) async-start(), calls=%async_computation.6 | async-start | bytes 4456448 | tf_op jit(solution)/shard_map/all_gather | solution.py:131
  131.5 106.7 %all-gather.11.cloned.1.call-start = ((), (), s32[]{:S(2)}) async-start(), calls=%async_computation.1 | async-start | bytes 2228224 | tf_op jit(solution)/shard_map/all_gather | solution.py:139
  144.0 129.8 %all-gather.15.cloned.1.call-start = ((), (), s32[]{:S(2)}) async-start(), calls=%async_computation.3 | async-start | bytes 2228224 | tf_op jit(solution)/shard_map/all_gather | solution.py:139
  150.1 159.5 %all-gather.19.cloned.1.call-start = ((), (), s32[]{:S(2)}) async-start(), calls=%async_computation.5 | async-start | bytes 2228224 | tf_op jit(solution)/shard_map/all_gather | solution.py:139
  169.6 175.8 %all-gather.23.cloned.1.call-start = ((), (), s32[]{:S(2)}) async-start(), calls=%async_computation.7 | async-start | bytes 2228224 | tf_op jit(solution)/shard_map/all_gather | solution.py:139
  202.6 6.7 %copy-start.4 = (s32[1,32]{1,0:T(1,128)S(1)}, s32[1,32]{1,0:T(1,128)}, u32[]{:S(2)}) copy-start(s32[1,32]{1,0:T(1,128)} %param.8) | copy-start | bytes 388
  202.6 10.9 %copy-start = (bf16[1,256,4096]{2,1,0:T(8,128)(2,1)S(1)}, bf16[1,256,4096]{2,1,0:T(8,128)(2,1)}, u32[]{:S(2)}) copy-start(bf16[1,256,4096]{2,1,0:T(8,128)(2,1)} %param.7) | copy-start | bytes 6291460
  345.5 33.6 %copy-start.1 = (bf16[256,1024]{1,0:T(8,128)(2,1)S(1)}, bf16[256,1024]{1,0:T(8,128)(2,1)}, u32[]{:S(2)}) copy-start(bf16[256,1024]{1,0:T(8,128)(2,1)} %shard_map.64) | copy-start | bytes 1572868
  345.5 33.6 %copy-start.2 = (bf16[256,1024]{1,0:T(8,128)(2,1)S(1)}, bf16[256,1024]{1,0:T(8,128)(2,1)}, u32[]{:S(2)}) copy-start(bf16[256,1024]{1,0:T(8,128)(2,1)} %shard_map.65) | copy-start | bytes 1572868
  345.5 33.6 %copy-start.3 = (bf16[256,1024]{1,0:T(8,128)(2,1)S(1)}, bf16[256,1024]{1,0:T(8,128)(2,1)}, u32[]{:S(2)}) copy-start(bf16[256,1024]{1,0:T(8,128)(2,1)} %shard_map.66) | copy-start | bytes 1572868
Sparse Core Ops, SparseCore 0:
  40.0 45.2 all-gather.8
  87.0 37.6 all-gather.12
  126.4 37.3 all-gather.16
  165.3 37.2 all-gather.20
  204.1 34.0 all-gather.10
  239.8 34.0 all-gather.14
  275.5 34.0 all-gather.18
  311.4 34.0 all-gather.22
